TPU v7x, 32 devices: a whole 2x2x4 slice. The times are simulated.
32 devices in a mesh: dp: 4 (over y, x), head: 8 (over z, core).
Axes of the slice: x: 2, y: 2, z: 4, core: 2. Of those that a mesh axis runs over, the one named last changes fastest.
Arguments:
- latents: bfloat16 [512, 512], P('dp'), may hold values from -6 to 6
- targets: bfloat16 [512, 32768], P('dp', 'head'), may hold values from -6 to 6
- kv_weight: bfloat16 [512, 32768], P(None, 'head'), may hold values from -0.25 to 0.25
- momentum: float32 [512, 8, 4096], P(None, 'head', 'dp'), may hold values from -120 to 120
Outputs:
- momentum_out: float32 [512, 8, 4096], P(None, 'head', 'dp')
- update: float32 [512, 8, 4096], P(None, 'head', 'dp')
All inputs are finite; a program needn't handle non-finite values.
Results may differ from a plain program's by a relative error of at most 0.0003.
The roundings to bfloat16 on the way count: a program that leaves them out, or rounds other values in their place, can miss the bound.
Values may be sent and summed in bfloat16 or wider, within the bound.
No kernel may reach another device: no remote copies, remote signals or barrier semaphores. Data moves between devices by JAX's collectives and lax.ppermute only.
A program may use at most 64 MiB of HBM per device.

v0:
```python
import math
import jax
import jax.numpy as jnp
from jax import lax
from jax.sharding import PartitionSpec as P

C = 32768
ITERS = 2
decay_rate = 0.95
linear_coef = 3.4445
square_coef = -4.775
quint_coef = 2.0315
epsilon = 1e-07


def gram_total(iterate):
    local_gram = lax.dot_general(
        iterate, iterate, (((1,), (1,)), ((), ())), precision=lax.Precision.HIGHEST
    )
    return lax.psum(local_gram, ("dp", "head"))


def local(latents, targets, kv_weight, momentum):
    latent_width = momentum.shape[0]
    sub_width = momentum.shape[2]
    total_tokens = latents.shape[0] * lax.axis_size("dp")
    residual = (
        jnp.dot(latents, kv_weight, preferred_element_type=jnp.float32)
        - targets.astype(jnp.float32)
    ).astype(jnp.bfloat16)
    columns = lax.all_to_all(residual, "dp", split_axis=1, concat_axis=0, tiled=True)
    gathered = lax.all_gather(latents, "dp", axis=0, tiled=True)
    gradient = lax.dot_general(
        gathered, columns, (((0,), (0,)), ((), ())), preferred_element_type=jnp.float32
    )
    gradient = gradient * (1.0 / math.sqrt(total_tokens))
    previous = momentum.reshape(latent_width, sub_width)
    momentum_new = decay_rate * previous + gradient
    nesterov = gradient + decay_rate * momentum_new
    squares = lax.psum(jnp.sum(nesterov * nesterov), ("dp", "head"))
    inverse = 1.0 / (jnp.sqrt(squares) + epsilon)
    iterate = nesterov * inverse
    gram_matrix = gram_total(iterate)
    for iteration in range(ITERS):
        if iteration > 0:
            gram_matrix = gram_total(iterate)
        polynomial = square_coef * gram_matrix + quint_coef * jnp.dot(
            gram_matrix, gram_matrix, precision=lax.Precision.HIGHEST
        )
        iterate = linear_coef * iterate + jnp.dot(
            polynomial, iterate, precision=lax.Precision.HIGHEST
        )
    update = iterate * math.sqrt(C)
    return (
        momentum_new.reshape(latent_width, 1, sub_width),
        update.reshape(latent_width, 1, sub_width),
    )


def solution(mesh):
    return jax.shard_map(
        local,
        mesh=mesh,
        in_specs=(P("dp", None), P("dp", "head"), P(None, "head"), P(None, "head", "dp")),
        out_specs=(P(None, "head", "dp"), P(None, "head", "dp")),
        check_vma=False,
    )
```

profile of v0, /device:TPU:0, one launch (start us, length us, event | category | flops | bytes accessed | tf_op | source)
XLA Modules:
  0.0 388.6 jit_solution(8422459653737256256)
XLA Ops:
  7.2 3.2 fusion
  10.4 0.0 copy-start.2
  10.4 1.0 copy.21
  11.5 5.2 %all-to-all-start = ((bf16[128,4,1024]{2,0,1:T(8,128)(2,1)}), bf16[128,4,1024]{2,0,1:T(8,128)(2,1)S(1)}, u32[]{:S(2)}, u32[]{:S(2)}) async-start(bf16[128,4,1024]{2,0,1:T(8,128)(2,1)} %bitcast.58), calls=%async_computation | async-start | bytes 2097152 | tf_op jit(solution)/shard_map/all_to_all | solution.py:31
  16.7 0.0 copy-start.3
  16.7 0.0 all-reduce.3.cloned.1.call-start
  16.7 0.0 copy-done.2
  16.7 4.4 %copy.11 = f32[512,1,1024]{0,2,1:T(8,128)} copy(f32[512,1,1024]{2,1,0:T(1,128)S(1)} %copy-done.2) | data formatting | bytes 4194304 | tf_op args[3]
  21.1 0.0 copy-done.3
  21.1 15.9 %all_gather.3 = bf16[512,512]{1,0:T(8,128)(2,1)} all-gather(bf16[128,512]{1,0:T(8,128)(2,1)S(1)} %copy-done.3), channel_id=1, replica_groups=mesh['dp'=4,'head'=8] {'dp'}, dimensions={0}, use_global_device_ids=true | all-gather | bytes 655360 | tf_op jit(solution)/shard_map/all_gather | solution.py:32
  37.0 0.0 all-to-all-done
  37.0 0.0 copy-start.1
  37.0 1.9 fusion.12
  38.9 0.0 copy-done.1
  38.9 0.0 copy-start
  38.9 2.6 multiply_reduce_fusion
  41.5 39.8 %psum.21 = f32[]{:T(128)} all-reduce(f32[]{:T(128)} %get-tuple-element.6), channel_id=1, replica_groups=mesh['dp'=4,'head'=8] {'dp','head'}, use_global_device_ids=true, to_apply=%region_1.0 | all-reduce | flops 1 | bytes 8 | tf_op jit(solution)/shard_map/psum | solution.py:40
  82.0 0.0 copy-done
  82.0 7.5 %fusion.3 = f32[512,512]{1,0:T(8,128)} fusion(f32[]{:T(128)S(6)} %div.3, f32[1024,512]{1,0:T(8,128)S(1)} %fusion.12, f32[512,1,1024]{0,2,1:T(8,128)} %copy.11), kind=kOutput, calls=%fused_computation.9 | convolution fusion | flops 3224371200 | bytes 5242884 | tf_op jit(solution)/shard_map/dot_general | solution.py:17
  89.4 0.0 all-reduce.3.cloned.1.call-update
  89.4 0.0 all-reduce.5.cloned.1.call-start
  89.5 130.9 %all-reduce.3.cloned.1.call-done = f32[512,512]{1,0:T(8,128)} async-done(((f32[512,512]{1,0:T(8,128)}), f32[512,512]{1,0:T(8,128)}) %all-reduce.3.cloned.1.call-update) | async-done | bytes 1048592 | tf_op jit(solution)/shard_map/psum | solution.py:20
  220.4 4.0 %fusion.9 = f32[512,512]{1,0:T(8,128)S(1)} fusion(f32[512,512]{1,0:T(8,128)} %all-reduce.3.cloned.1.call-done), kind=kOutput, calls=%fused_computation.15 | convolution fusion | flops 1611399168 | bytes 2097152 | tf_op jit(solution)/shard_map/dot_general | solution.py:47
  224.4 8.1 %multiply_add_fusion = f32[512,1024]{0,1:T(8,128)S(1)} fusion(f32[512,512]{1,0:T(8,128)S(1)} %fusion.9, f32[]{:T(128)S(6)} %div.3, f32[512,1,1024]{0,2,1:T(8,128)} %copy.11, f32[1024,512]{1,0:T(8,128)} %copy-done), kind=kOutput, calls=%fused_computation.5 | convolution fusion | flops 3228565504 | bytes 7340036 | tf_op jit(solution)/shard_map/dot_general | solution.py:50
  232.5 4.5 %fusion.13 = f32[512,512]{1,0:T(8,128)} fusion(f32[512,1024]{0,1:T(8,128)S(1)} %multiply_add_fusion), kind=kOutput, calls=%fused_computation.20 | convolution fusion | flops 3221225472 | bytes 3145728 | tf_op jit(solution)/shard_map/dot_general | solution.py:17
  237.0 0.0 all-reduce.5.cloned.1.call-update
  237.0 6.0 %copy.15 = f32[512,1,1024]{2,1,0:T(1,128)} copy(f32[512,1,1024]{0,2,1:T(8,128)} %get-tuple-element.7) | data formatting | bytes 4194304
  243.1 123.7 %all-reduce.5.cloned.1.call-done = f32[512,512]{1,0:T(8,128)} async-done(((f32[512,512]{1,0:T(8,128)}), f32[512,512]{1,0:T(8,128)}) %all-reduce.5.cloned.1.call-update) | async-done | bytes 1048592 | tf_op jit(solution)/shard_map/psum | solution.py:20
  366.8 4.0 %fusion.8 = f32[512,512]{1,0:T(8,128)S(1)} fusion(f32[512,512]{1,0:T(8,128)} %all-reduce.5.cloned.1.call-done), kind=kOutput, calls=%fused_computation.13 | convolution fusion | flops 1611399168 | bytes 2097152 | tf_op jit(solution)/shard_map/dot_general | solution.py:47
  370.8 4.9 %multiply_bitcast_fusion = f32[512,1,1024]{0,2,1:T(8,128)} fusion(f32[512,1024]{0,1:T(8,128)S(1)} %multiply_add_fusion, f32[512,512]{1,0:T(8,128)S(1)} %fusion.8), kind=kOutput, calls=%fused_computation.4 | convolution fusion | flops 3222798336 | bytes 5242880 | tf_op jit(solution)/shard_map/dot_general | solution.py:50
  375.8 6.0 %copy.16 = f32[512,1,1024]{2,1,0:T(1,128)} copy(f32[512,1,1024]{0,2,1:T(8,128)} %multiply_bitcast_fusion) | data formatting | bytes 4194304
Async XLA Ops:
  10.4 6.2 %copy-start.2 = (f32[512,1,1024]{2,1,0:T(1,128)S(1)}, f32[512,1,1024]{2,1,0:T(1,128)}, u32[]{:S(2)}) copy-start(f32[512,1,1024]{2,1,0:T(1,128)} %param.7) | copy-start | bytes 6291460
  11.5 25.5 %all-to-all-start = ((bf16[128,4,1024]{2,0,1:T(8,128)(2,1)}), bf16[128,4,1024]{2,0,1:T(8,128)(2,1)S(1)}, u32[]{:S(2)}, u32[]{:S(2)}) async-start(bf16[128,4,1024]{2,0,1:T(8,128)(2,1)} %bitcast.58), calls=%async_computation | async-start | bytes 2097152 | tf_op jit(solution)/shard_map/all_to_all | solution.py:31
  16.7 4.4 %copy-start.3 = (bf16[128,512]{1,0:T(8,128)(2,1)S(1)}, bf16[128,512]{1,0:T(8,128)(2,1)}, u32[]{:S(2)}) copy-start(bf16[128,512]{1,0:T(8,128)(2,1)} %param.4) | copy-start | bytes 393220
  16.7 203.7 %all-reduce.3.cloned.1.call-start = ((), (), s32[]{:S(2)}) async-start(), calls=%async_computation.1 | async-start | bytes 2097152 | tf_op jit(solution)/shard_map/psum | solution.py:20
  37.0 1.9 copy-start.1
  38.9 43.0 %copy-start = (f32[1024,512]{1,0:T(8,128)}, f32[1024,512]{1,0:T(8,128)S(1)}, u32[]{:S(2)}) copy-start(f32[1024,512]{1,0:T(8,128)S(1)} %fusion.12) | copy-start | bytes 6291460
  89.4 277.4 %all-reduce.5.cloned.1.call-start = ((), (), s32[]{:S(2)}) async-start(), calls=%async_computation.2 | async-start | bytes 2097152 | tf_op jit(solution)/shard_map/psum | solution.py:20
Sparse Core Ops, SparseCore 0:
  89.6 130.7 all-reduce.2
  237.1 129.6 all-reduce.4
where the time goes:
time: 389 us
  waiting for transfers between devices  255 us (66%)
  blocking collectives  55.6 us (14%)
  matrix products  38.2 us (10%)
  local copies, waits for them, and re-layouts  17.5 us (4%)
  between operations  14.7 us (4%)
  starting transfers between devices  5.24 us (1%)
    psum x2, waiting for transfers between devices, gram_total(): return lax.psum(local_gram, ('dp', 'head'))  255 us
    psum x1, blocking collectives, local(): squares = lax.psum(jnp.sum(nesterov * nesterov), ('dp', 'head'))  39.8 us
    unnamed x11, local copies, waits for them, and re-layouts  16.5 us
    all_gather x1, blocking collectives, local(): gathered = lax.all_gather(latents, 'dp', axis=0, tiled=True)  15.9 us
    dot_general x2, matrix products, local(): jnp.dot(polynomial, iterate, precision=lax.Precision.HIGHEST)  13 us
    dot_general x2, matrix products, gram_total(): lax.dot_general(iterate, iterate, (((1,), (1,)), ((), ())), precision=lax...  11.9 us
    dot_general x2, matrix products, local(): jnp.dot(gram_matrix, gram_matrix, precision=lax.Precision.HIGHEST)  8.05 us
  transfers between devices with their start and end apart: 3, of which 2 were waited for; matrix products, arithmetic and copies ran while one was open for 3% of the time, Pallas kernels for 0%

commit v1 on v0

--- a/solution.py
+++ b/solution.py
@@ -13,11 +13,17 @@
 epsilon = 1e-07
 
 
+def summed_here(x, mesh_axis):
+    pieces = lax.all_gather(x, mesh_axis, axis=0, tiled=False)
+    total = pieces.sum(axis=0)
+    return total
+
+
 def gram_total(iterate):
     local_gram = lax.dot_general(
         iterate, iterate, (((1,), (1,)), ((), ())), precision=lax.Precision.HIGHEST
     )
-    return lax.psum(local_gram, ("dp", "head"))
+    return summed_here(local_gram, ("dp", "head"))
 
 
 def local(latents, targets, kv_weight, momentum):

time: 389 us -> 535 us (1.38)
  waiting for transfers between devices: 255 us -> 381 us
  other arithmetic: 2.63 us -> 27.4 us
  matrix products: 38.2 us -> 32.2 us
    all_gather x0 -> x2, waiting for transfers between devices: none -> 381 us  [summed_here(): pieces = lax.all_gather(x, mesh_axis, axis=0, tiled=False)]
    psum x2 -> x0, waiting for transfers between devices: 255 us -> none  [gram_total(): return lax.psum(local_gram, ('dp', 'head'))]
    reduce_sum x0 -> x2, other arithmetic: none -> 24.8 us  [summed_here(): total = pieces.sum(axis=0)]
    unnamed x11 -> x13, local copies, waits for them, and re-layouts: 16.5 us -> 16.5 us
  transfers between devices with their start and end apart: 3 -> 3, of which waited for: 2 -> 2; matrix products, arithmetic and copies ran while one was open for 3% -> 2% of each run, Pallas kernels for 0% -> 0%
where the time goes in v1:
time: 535 us; the launch traced here: 534 us
  waiting for transfers between devices  381 us (71%)
  blocking collectives  55.6 us (10%)
  matrix products  32.2 us (6%)
  other arithmetic  27.4 us (5%)
  local copies, waits for them, and re-layouts  17.5 us (3%)
  between operations  14.8 us (3%)
  starting transfers between devices  5.42 us (1%)
    all_gather x2, waiting for transfers between devices, summed_here(): pieces = lax.all_gather(x, mesh_axis, axis=0, tiled=False)  381 us
    psum x1, blocking collectives, local(): squares = lax.psum(jnp.sum(nesterov * nesterov), ('dp', 'head'))  39.7 us
    reduce_sum x2, other arithmetic, summed_here(): total = pieces.sum(axis=0)  24.8 us
    unnamed x13, local copies, waits for them, and re-layouts  16.5 us
    all_gather x1, blocking collectives, local(): gathered = lax.all_gather(latents, 'dp', axis=0, tiled=True)  15.9 us
    dot_general x2, matrix products, gram_total(): lax.dot_general(iterate, iterate, (((1,), (1,)), ((), ())), precision=lax...  11.9 us
    dot_general x2, matrix products, local(): jnp.dot(polynomial, iterate, precision=lax.Precision.HIGHEST)  11.3 us
  transfers between devices with their start and end apart: 3, of which 2 were waited for; matrix products, arithmetic and copies ran while one was open for 2% of the time, Pallas kernels for 0%

profile of v1, /device:TPU:0, one launch (start us, length us, event | category | flops | bytes accessed | tf_op | source)
XLA Modules:
  0.0 533.8 jit_solution(2059428106916003486)
XLA Ops:
  7.2 3.2 fusion
  10.4 0.0 copy-start.3
  10.4 1.0 copy.21
  11.5 5.2 all-to-all-start
  16.7 0.0 all-gather.5.cloned.1.call-start
  16.7 0.0 copy-done.3
  16.7 4.4 copy.11
  21.1 0.0 copy-done.4
  21.1 15.9 %all_gather.15 = bf16[512,512]{1,0:T(8,128)(2,1)} all-gather(bf16[128,512]{1,0:T(8,128)(2,1)S(1)} %copy-done.4), channel_id=1, replica_groups=mesh['dp'=4,'head'=8] {'dp'}, dimensions={0}, use_global_device_ids=true | all-gather | bytes 655360 | tf_op jit(solution)/shard_map/all_gather | solution.py:38
  37.0 0.0 all-to-all-done
  37.0 1.9 fusion.12
  38.9 0.0 copy-done.2
  38.9 0.0 copy-start
  38.9 2.6 multiply_reduce_fusion
  41.6 39.7 %psum.7 = f32[]{:T(128)} all-reduce(f32[]{:T(128)} %get-tuple-element.6), channel_id=1, replica_groups=mesh['dp'=4,'head'=8] {'dp','head'}, use_global_device_ids=true, to_apply=%region_1.0 | all-reduce | flops 1 | bytes 8 | tf_op jit(solution)/shard_map/psum | solution.py:46
  82.0 0.0 copy-done
  82.0 7.5 %fusion.3 = f32[512,512]{1,0:T(8,128)} fusion(f32[]{:T(128)S(6)} %div.3, f32[1024,512]{1,0:T(8,128)S(1)} %fusion.12, f32[512,1,1024]{0,2,1:T(8,128)} %copy.11), kind=kOutput, calls=%fused_computation.9 | convolution fusion | flops 3224371200 | bytes 5242884 | tf_op jit(solution)/shard_map/dot_general | solution.py:23
  89.5 0.0 all-gather.5.cloned.1.call-update
  89.5 0.2 all-gather.7.cloned.1.call-start
  89.7 194.3 %all-gather.5.cloned.1.call-done = f32[16384,512]{1,0:T(8,128)} async-done(((f32[512,512]{1,0:T(8,128)}), f32[16384,512]{1,0:T(8,128)}) %all-gather.5.cloned.1.call-update) | async-done | bytes 33554448 | tf_op jit(solution)/shard_map/all_gather | solution.py:17
  284.1 12.3 %reduce_sum.28 = f32[512,512]{1,0:T(8,128)S(1)} reduce(f32[32,512,512]{2,1,0:T(8,128)} %bitcast.62, f32[]{:T(128)} %constant.3.clone.1), dimensions={0}, to_apply=%region_2.0 | reduce | flops 8126464 | bytes 34603012 | tf_op jit(solution)/shard_map/reduce_sum | solution.py:18
  296.4 0.0 copy-start.1
  296.4 1.9 fusion.9
  298.3 6.3 %multiply_add_fusion = f32[512,1024]{0,1:T(8,128)S(1)} fusion(f32[512,512]{1,0:T(8,128)S(1)} %fusion.9, f32[]{:T(128)S(6)} %div.3, f32[512,1,1024]{0,2,1:T(8,128)} %copy.11, f32[1024,512]{1,0:T(8,128)S(1)} %copy-done.1), kind=kOutput, calls=%fused_computation.5 | convolution fusion | flops 3228565504 | bytes 7340036 | tf_op jit(solution)/shard_map/dot_general | solution.py:56
  304.6 4.5 fusion.13
  309.1 0.0 all-gather.7.cloned.1.call-update
  309.2 6.0 %copy.15 = f32[512,1,1024]{2,1,0:T(1,128)} copy(f32[512,1,1024]{0,2,1:T(8,128)} %get-tuple-element.7) | data formatting | bytes 4194304
  315.2 186.5 %all-gather.7.cloned.1.call-done = f32[16384,512]{1,0:T(8,128)} async-done(((f32[512,512]{1,0:T(8,128)}), f32[16384,512]{1,0:T(8,128)}) %all-gather.7.cloned.1.call-update) | async-done | bytes 33554448 | tf_op jit(solution)/shard_map/all_gather | solution.py:17
  501.7 12.5 %reduce_sum.29 = f32[512,512]{1,0:T(8,128)S(1)} reduce(f32[32,512,512]{2,1,0:T(8,128)} %bitcast.61, f32[]{:T(128)} %constant.3.clone.1), dimensions={0}, to_apply=%region_3.0 | reduce | flops 8126464 | bytes 34603012 | tf_op jit(solution)/shard_map/reduce_sum | solution.py:18
  514.2 1.9 fusion.8
  516.1 4.9 multiply_bitcast_fusion
  521.0 6.0 %copy.16 = f32[512,1,1024]{2,1,0:T(1,128)} copy(f32[512,1,1024]{0,2,1:T(8,128)} %multiply_bitcast_fusion) | data formatting | bytes 4194304
  (3 shorter events, 0.0 us)
Async XLA Ops:
  10.4 6.2 %copy-start.3 = (f32[512,1,1024]{2,1,0:T(1,128)S(1)}, f32[512,1,1024]{2,1,0:T(1,128)}, u32[]{:S(2)}) copy-start(f32[512,1,1024]{2,1,0:T(1,128)} %param.7) | copy-start | bytes 6291460
  11.5 25.5 %all-to-all-start = ((bf16[128,4,1024]{2,0,1:T(8,128)(2,1)}), bf16[128,4,1024]{2,0,1:T(8,128)(2,1)S(1)}, u32[]{:S(2)}, u32[]{:S(2)}) async-start(bf16[128,4,1024]{2,0,1:T(8,128)(2,1)} %bitcast.60), calls=%async_computation | async-start | bytes 2097152 | tf_op jit(solution)/shard_map/all_to_all | solution.py:37
  16.7 4.4 copy-start.4
  16.7 267.4 %all-gather.5.cloned.1.call-start = ((), (), s32[]{:S(2)}) async-start(), calls=%async_computation.1 | async-start | bytes 34603008 | tf_op jit(solution)/shard_map/all_gather | solution.py:17
  37.0 1.9 copy-start.2
  38.9 43.1 %copy-start = (f32[1024,512]{1,0:T(8,128)}, f32[1024,512]{1,0:T(8,128)S(1)}, u32[]{:S(2)}) copy-start(f32[1024,512]{1,0:T(8,128)S(1)} %fusion.12) | copy-start | bytes 6291460
  89.5 412.2 %all-gather.7.cloned.1.call-start = ((), (), s32[]{:S(2)}) async-start(), calls=%async_computation.2 | async-start | bytes 34603008 | tf_op jit(solution)/shard_map/all_gather | solution.py:17
  296.4 1.9 copy-start.1
Sparse Core Ops, SparseCore 0:
  89.6 194.4 all-gather.4
  309.3 192.3 all-gather.6
